TPU v7x, 256 devices: a whole 4x4x8 slice. The times are simulated.
256 devices in a mesh: pix: 64 (over z, y, core), band: 4 (over x).
Axes of the slice: x: 4, y: 4, z: 8, core: 2. Of those that a mesh axis runs over, the one named last changes fastest.
Arguments:
- series: bfloat16 [224, 128, 16384], P('band', None, 'pix'), may hold values from 0 to 1
- pixel_factor: float32 [64, 16384], P(None, 'pix'), may hold values from 0.03 to 0.6
- band_factor: float32 [224, 64], P('band'), may hold values from 0.03 to 0.6
- time_factor: float32 [128, 64], replicated, may hold values from 0.03 to 0.6
Outputs:
- pixels_out: float32 [64, 16384], P(None, 'pix')
- bands_out: float32 [224, 64], P('band')
- times_out: float32 [128, 64], replicated
All inputs are finite; a program needn't handle non-finite values.
Results may differ from a plain program's by a relative error of at most 0.00045.
Values sent between devices are 32-bit elements; how exact they have to be, the bound alone decides.
A program may use at most 64 MiB of HBM per device.

v0:
```python
import jax
import jax.numpy as jnp
from jax import lax
from jax.sharding import PartitionSpec as P

SWEEPS = 4
HIGH = lax.Precision.HIGHEST


def step_of(gram):
    return 1.0 / (jnp.max(jnp.sum(gram, axis=1)) + 1e-06)


def band_gram_of(bands):
    local_gram = jnp.dot(bands.T, bands, precision=HIGH, preferred_element_type=jnp.float32)
    return lax.psum(local_gram, "band")


def body(series, pixel_factor, band_factor, time_factor):
    pixels = pixel_factor
    bands = band_factor
    times = time_factor
    gram_b = band_gram_of(bands)
    for sweep in range(SWEEPS):
        gram_c = jnp.dot(times.T, times, precision=HIGH, preferred_element_type=jnp.float32)
        c_low = times.astype(jnp.bfloat16)
        folded = jnp.einsum("btp,tr->brp", series, c_low, preferred_element_type=jnp.float32)
        partial_a = jnp.einsum("brp,br->rp", folded, bands, precision=HIGH)
        gram = gram_b * gram_c
        scale = step_of(gram)
        target = lax.psum(partial_a, "band")
        pixels = jnp.maximum(pixels - scale * (jnp.dot(gram, pixels, precision=HIGH) - target), 0.0)
        local_gram = jnp.dot(pixels, pixels.T, precision=HIGH, preferred_element_type=jnp.float32)
        partial_b = jnp.einsum("brp,rp->br", folded, pixels, precision=HIGH)
        gram_a = lax.psum(local_gram, "pix")
        target_b = lax.psum(partial_b, "pix")
        gram = gram_a * gram_c
        bands = jnp.maximum(
            bands - step_of(gram) * (jnp.dot(bands, gram, precision=HIGH) - target_b), 0.0
        )
        gram_b = band_gram_of(bands)
        p_low = pixels.astype(jnp.bfloat16)
        b_low = bands.astype(jnp.bfloat16).astype(jnp.float32)
        spread = jnp.einsum("btp,rp->brt", series, p_low, preferred_element_type=jnp.float32)
        partial_c = jnp.einsum("brt,br->tr", spread, b_low, precision=HIGH)
        target_c = lax.psum(partial_c, ("pix", "band"))
        gram = gram_a * gram_b
        times = jnp.maximum(
            times - step_of(gram) * (jnp.dot(times, gram, precision=HIGH) - target_c), 0.0
        )
    return (pixels, bands, times)


def solution(mesh):
    placed = (P("band", None, "pix"), P(None, "pix"), P("band", None), P())
    return jax.shard_map(
        body,
        mesh=mesh,
        in_specs=placed,
        out_specs=(P(None, "pix"), P("band", None), P()),
        check_vma=False,
    )
```

profile of v0, /device:TPU:32, one launch (start us, length us, event | category | flops | bytes accessed | tf_op | source)
XLA Modules:
  0.0 1637.9 jit_solution(12999607043672692766)
XLA Ops:
  8.0 2.7 convolution_bitcast_fusion.3
  12.5 4.1 fusion.14
  17.8 17.1 %psum.147 = f32[64,64]{1,0:T(8,128)S(1)} all-reduce(f32[64,64]{1,0:T(8,128)S(1)} %fusion.102), channel_id=1, replica_groups=mesh['pix'=64,'band'=4] {'band'}, use_global_device_ids=true, to_apply=%region_0.0 | all-reduce | flops 4096 | bytes 32768 | tf_op jit(solution)/shard_map/psum | solution.py:16
  36.4 29.6 %all-reduce.9.cloned.1.call-done = f32[64,256]{1,0:T(8,128)} async-done(((f32[64,256]{1,0:T(8,128)}), f32[64,256]{1,0:T(8,128)}) %all-reduce.9.cloned.1.call-update) | async-done | bytes 65552 | tf_op jit(solution)/shard_map/psum | solution.py:31
  67.3 3.3 fusion.76
  70.6 4.9 fusion.12
  75.6 231.5 %all-reduce.3 = (f32[56,64]{1,0:T(8,128)S(1)}, f32[64,64]{0,1:T(8,128)S(1)}) all-reduce(f32[56,64]{1,0:T(8,128)S(1)} %bitcast.190, f32[64,64]{0,1:T(8,128)S(1)} %fusion.104), channel_id=1, replica_groups=mesh['pix'=64,'band'=4] {'pix'}, use_global_device_ids=true, to_apply=%region_7.0 | all-reduce | flops 7680 | bytes 61440 | tf_op jit(solution)/shard_map/psum | solution.py:36
  311.1 91.0 %psum.152 = f32[128,64]{0,1:T(8,128)S(1)} all-reduce(f32[128,64]{0,1:T(8,128)S(1)} %bitcast.186), channel_id=1, replica_groups=mesh['pix'=64,'band'=4] {'pix','band'}, use_global_device_ids=true, to_apply=%region_11.0 | all-reduce | flops 8192 | bytes 65536 | tf_op jit(solution)/shard_map/psum | solution.py:46
  402.1 15.7 psum.151
  419.3 2.7 convolution_bitcast_fusion.2
  423.8 4.1 fusion.10
  430.4 39.1 %all-reduce.11.cloned.1.call-done = f32[64,256]{1,0:T(8,128)} async-done(((f32[64,256]{1,0:T(8,128)}), f32[64,256]{1,0:T(8,128)}) %all-reduce.11.cloned.1.call-update) | async-done | bytes 65552 | tf_op jit(solution)/shard_map/psum | solution.py:31
  471.0 3.3 fusion.74
  474.3 4.9 fusion.8
  479.3 231.3 %all-reduce.2 = (f32[56,64]{1,0:T(8,128)S(1)}, f32[64,64]{0,1:T(8,128)S(1)}) all-reduce(f32[56,64]{1,0:T(8,128)S(1)} %bitcast.191, f32[64,64]{0,1:T(8,128)S(1)} %fusion.106), channel_id=1, replica_groups=mesh['pix'=64,'band'=4] {'pix'}, use_global_device_ids=true, to_apply=%region_18.0 | all-reduce | flops 7680 | bytes 61440 | tf_op jit(solution)/shard_map/psum | solution.py:36
  714.5 91.0 %psum.157 = f32[128,64]{0,1:T(8,128)S(1)} all-reduce(f32[128,64]{0,1:T(8,128)S(1)} %bitcast.187), channel_id=1, replica_groups=mesh['pix'=64,'band'=4] {'pix','band'}, use_global_device_ids=true, to_apply=%region_22.0 | all-reduce | flops 8192 | bytes 65536 | tf_op jit(solution)/shard_map/psum | solution.py:46
  805.5 16.0 psum.156
  823.0 2.7 convolution_bitcast_fusion.1
  827.4 4.1 fusion.6
  833.7 39.6 %all-reduce.13.cloned.1.call-done = f32[64,256]{1,0:T(8,128)} async-done(((f32[64,256]{1,0:T(8,128)}), f32[64,256]{1,0:T(8,128)}) %all-reduce.13.cloned.1.call-update) | async-done | bytes 65552 | tf_op jit(solution)/shard_map/psum | solution.py:31
  874.7 3.3 fusion.72
  878.0 4.9 fusion.4
  883.0 231.5 %all-reduce.1 = (f32[56,64]{1,0:T(8,128)S(1)}, f32[64,64]{0,1:T(8,128)S(1)}) all-reduce(f32[56,64]{1,0:T(8,128)S(1)} %bitcast.192, f32[64,64]{0,1:T(8,128)S(1)} %fusion.108), channel_id=1, replica_groups=mesh['pix'=64,'band'=4] {'pix'}, use_global_device_ids=true, to_apply=%region_29.0 | all-reduce | flops 7680 | bytes 61440 | tf_op jit(solution)/shard_map/psum | solution.py:36
  1118.5 91.0 %psum.162 = f32[128,64]{0,1:T(8,128)S(1)} all-reduce(f32[128,64]{0,1:T(8,128)S(1)} %bitcast.188), channel_id=1, replica_groups=mesh['pix'=64,'band'=4] {'pix','band'}, use_global_device_ids=true, to_apply=%region_33.0 | all-reduce | flops 8192 | bytes 65536 | tf_op jit(solution)/shard_map/psum | solution.py:46
  1209.5 15.7 psum.161
  1231.2 4.1 fusion.2
  1237.4 39.5 %all-reduce.15.cloned.1.call-done = f32[64,256]{1,0:T(8,128)} async-done(((f32[64,256]{1,0:T(8,128)}), f32[64,256]{1,0:T(8,128)}) %all-reduce.15.cloned.1.call-update) | async-done | bytes 65552 | tf_op jit(solution)/shard_map/psum | solution.py:31
  1278.4 3.3 fusion.70
  1281.7 4.9 fusion
  1286.7 231.6 %all-reduce = (f32[56,64]{1,0:T(8,128)S(1)}, f32[64,64]{0,1:T(8,128)S(1)}) all-reduce(f32[56,64]{1,0:T(8,128)S(1)} %bitcast.193, f32[64,64]{0,1:T(8,128)S(1)} %fusion.110), channel_id=1, replica_groups=mesh['pix'=64,'band'=4] {'pix'}, use_global_device_ids=true, to_apply=%region_40.0 | all-reduce | flops 7680 | bytes 61440 | tf_op jit(solution)/shard_map/psum | solution.py:36
  1522.1 91.0 %psum.167 = f32[128,64]{0,1:T(8,128)S(1)} all-reduce(f32[128,64]{0,1:T(8,128)S(1)} %bitcast.189), channel_id=1, replica_groups=mesh['pix'=64,'band'=4] {'pix','band'}, use_global_device_ids=true, to_apply=%region_44.0 | all-reduce | flops 8192 | bytes 65536 | tf_op jit(solution)/shard_map/psum | solution.py:46
  1613.1 15.7 psum.166
  (106 shorter events, 40.2 us)
Async XLA Ops:
  7.2 58.8 %all-reduce.9.cloned.1.call-start = ((), (), s32[]{:S(2)}) async-start(), calls=%async_computation | async-start | bytes 131072 | tf_op jit(solution)/shard_map/psum | solution.py:31
  10.7 1.8 copy-start
  12.5 4.8 copy-start.10
  12.5 5.0 copy-start.9
  12.5 53.4 %copy-start.12 = (f32[64,256]{1,0:T(8,128)S(1)}, f32[64,256]{1,0:T(8,128)}, u32[]{:S(2)}) copy-start(f32[64,256]{1,0:T(8,128)} %param.5) | copy-start | bytes 196612
  17.3 452.2 %all-reduce.11.cloned.1.call-start = ((), (), s32[]{:S(2)}) async-start(), calls=%async_computation.1 | async-start | bytes 131072 | tf_op jit(solution)/shard_map/psum | solution.py:31
  65.9 4.7 copy-start.1
  422.0 1.8 copy-start.2
  428.5 444.8 %all-reduce.13.cloned.1.call-start = ((), (), s32[]{:S(2)}) async-start(), calls=%async_computation.2 | async-start | bytes 131072 | tf_op jit(solution)/shard_map/psum | solution.py:31
  469.5 4.7 copy-start.3
  825.6 1.8 copy-start.4
  832.2 444.8 %all-reduce.15.cloned.1.call-start = ((), (), s32[]{:S(2)}) async-start(), calls=%async_computation.3 | async-start | bytes 131072 | tf_op jit(solution)/shard_map/psum | solution.py:31
  873.3 4.7 copy-start.5
  1229.4 1.8 copy-start.6
  1276.9 4.7 copy-start.7
  1278.2 8.4 copy-start.8
  1519.8 111.1 %copy-start.11 = (f32[56,64]{1,0:T(8,128)}, f32[56,64]{1,0:T(8,128)S(1)}, u32[]{:S(2)}) copy-start(f32[56,64]{1,0:T(8,128)S(1)} %fusion.55) | copy-start | bytes 43012
Sparse Core Ops, SparseCore 0:
  17.4 48.4 all-reduce.8
  428.6 40.8 all-reduce.10
  832.3 40.9 all-reduce.12
  1236.0 40.8 all-reduce.14
where the time goes:
time: 1650 us; the launch traced here: 1640 us
  blocking collectives  1370 us (83%)
  waiting for transfers between devices  148 us (9%)
  matrix products  77.5 us (5%)
  between operations  22.9 us (1%)
    psum x4, blocking collectives, body(): target_b = lax.psum(partial_b, 'pix')  926 us
    psum x4, blocking collectives, body(): target_c = lax.psum(partial_c, ('pix', 'band'))  364 us
    psum x4, waiting for transfers between devices, body(): target = lax.psum(partial_a, 'band')  148 us
    psum x5, blocking collectives, band_gram_of(): return lax.psum(local_gram, 'band')  80.2 us
  transfers between devices with their start and end apart: 4, of which 4 were waited for; matrix products, arithmetic and copies ran while one was open for 0% of the time, Pallas kernels for 0%

commit v1 on v0

--- a/solution.py
+++ b/solution.py
@@ -43,7 +43,7 @@
         b_low = bands.astype(jnp.bfloat16).astype(jnp.float32)
         spread = jnp.einsum("btp,rp->brt", series, p_low, preferred_element_type=jnp.float32)
         partial_c = jnp.einsum("brt,br->tr", spread, b_low, precision=HIGH)
-        target_c = lax.psum(partial_c, ("pix", "band"))
+        target_c = jnp.sum(lax.all_gather(partial_c, ("pix", "band")), axis=0)
         gram = gram_a * gram_b
         times = jnp.maximum(
             times - step_of(gram) * (jnp.dot(times, gram, precision=HIGH) - target_c), 0.0

time: 1650 us -> 1770 us (1.073)
  waiting for transfers between devices: 148 us -> 614 us
  blocking collectives: 1370 us -> 1010 us
  local copies, waits for them, and re-layouts: 11.6 us -> 33.3 us
    all_gather x0 -> x4, waiting for transfers between devices: none -> 454 us  [body(): target_c = jnp.sum(lax.all_gather(partial_c, ('pix', 'band')), axis=0)]
    psum x4 -> x0, blocking collectives: 364 us -> none  [body(): target_c = lax.psum(partial_c, ('pix', 'band'))]
    unnamed x27 -> x37, local copies, waits for them, and re-layouts: 8.02 us -> 29.8 us
  transfers between devices with their start and end apart: 4 -> 8, of which waited for: 4 -> 8; matrix products, arithmetic and copies ran while one was open for 0% -> 0% of each run, Pallas kernels for 0% -> 0%
where the time goes in v1:
time: 1770 us; the launch traced here: 1760 us
  blocking collectives  1010 us (57%)
  waiting for transfers between devices  614 us (35%)
  matrix products  73.8 us (4%)
  local copies, waits for them, and re-layouts  33.3 us (2%)
  between operations  23.3 us (1%)
    psum x4, blocking collectives, body(): target_b = lax.psum(partial_b, 'pix')  925 us
    all_gather x4, waiting for transfers between devices, body(): target_c = jnp.sum(lax.all_gather(partial_c, ('pix', 'band')), axis=0)  454 us
    psum x4, waiting for transfers between devices, body(): target = lax.psum(partial_a, 'band')  160 us
    psum x5, blocking collectives, band_gram_of(): return lax.psum(local_gram, 'band')  81.6 us
  transfers between devices with their start and end apart: 8, of which 8 were waited for; matrix products, arithmetic and copies ran while one was open for 0% of the time, Pallas kernels for 0%

profile of v1, /device:TPU:32, one launch (start us, length us, event | category | flops | bytes accessed | tf_op | source)
XLA Modules:
  0.0 1764.3 jit_solution(15109588421422133261)
XLA Ops:
  12.5 4.1 fusion.14
  17.8 17.1 psum.119
  36.4 29.6 %all-reduce.9.cloned.1.call-done = f32[64,256]{1,0:T(8,128)} async-done(((f32[64,256]{1,0:T(8,128)}), f32[64,256]{1,0:T(8,128)}) %all-reduce.9.cloned.1.call-update) | async-done | bytes 65552 | tf_op jit(solution)/shard_map/psum | solution.py:31
  67.3 3.3 fusion.76
  70.6 4.9 fusion.12
  75.6 231.5 %all-reduce.3 = (f32[56,64]{1,0:T(8,128)S(1)}, f32[64,64]{0,1:T(8,128)S(1)}) all-reduce(f32[56,64]{1,0:T(8,128)S(1)} %bitcast.214, f32[64,64]{0,1:T(8,128)S(1)} %fusion.104), channel_id=1, replica_groups=mesh['pix'=64,'band'=4] {'pix'}, use_global_device_ids=true, to_apply=%region_7.0 | all-reduce | flops 7680 | bytes 61440 | tf_op jit(solution)/shard_map/psum | solution.py:36
  311.8 16.0 psum.123
  329.1 113.5 %all-gather.9.cloned.1.call-done = f32[32768,64]{0,1:T(8,128)} async-done(((f32[128,64]{0,1:T(8,128)}), f32[32768,64]{0,1:T(8,128)}) %all-gather.9.cloned.1.call-update) | async-done | bytes 8388624 | tf_op jit(solution)/shard_map/all_gather | solution.py:46
  442.6 4.9 copy.65
  451.9 4.1 fusion.10
  458.6 43.4 %all-reduce.11.cloned.1.call-done = f32[64,256]{1,0:T(8,128)} async-done(((f32[64,256]{1,0:T(8,128)}), f32[64,256]{1,0:T(8,128)}) %all-reduce.11.cloned.1.call-update) | async-done | bytes 65552 | tf_op jit(solution)/shard_map/psum | solution.py:31
  503.4 3.3 fusion.74
  506.7 4.9 fusion.8
  511.7 231.3 %all-reduce.2 = (f32[56,64]{1,0:T(8,128)S(1)}, f32[64,64]{0,1:T(8,128)S(1)}) all-reduce(f32[56,64]{1,0:T(8,128)S(1)} %bitcast.215, f32[64,64]{0,1:T(8,128)S(1)} %fusion.106), channel_id=1, replica_groups=mesh['pix'=64,'band'=4] {'pix'}, use_global_device_ids=true, to_apply=%region_18.0 | all-reduce | flops 7680 | bytes 61440 | tf_op jit(solution)/shard_map/psum | solution.py:36
  747.6 16.2 psum.127
  765.2 113.2 %all-gather.11.cloned.1.call-done = f32[32768,64]{0,1:T(8,128)} async-done(((f32[128,64]{0,1:T(8,128)}), f32[32768,64]{0,1:T(8,128)}) %all-gather.11.cloned.1.call-update) | async-done | bytes 8388624 | tf_op jit(solution)/shard_map/all_gather | solution.py:46
  878.5 4.9 copy.66
  887.8 4.1 fusion.6
  894.3 43.5 %all-reduce.13.cloned.1.call-done = f32[64,256]{1,0:T(8,128)} async-done(((f32[64,256]{1,0:T(8,128)}), f32[64,256]{1,0:T(8,128)}) %all-reduce.13.cloned.1.call-update) | async-done | bytes 65552 | tf_op jit(solution)/shard_map/psum | solution.py:31
  939.3 3.3 fusion.72
  942.6 4.9 fusion.4
  947.6 231.3 %all-reduce.1 = (f32[56,64]{1,0:T(8,128)S(1)}, f32[64,64]{0,1:T(8,128)S(1)}) all-reduce(f32[56,64]{1,0:T(8,128)S(1)} %bitcast.216, f32[64,64]{0,1:T(8,128)S(1)} %fusion.108), channel_id=1, replica_groups=mesh['pix'=64,'band'=4] {'pix'}, use_global_device_ids=true, to_apply=%region_29.0 | all-reduce | flops 7680 | bytes 61440 | tf_op jit(solution)/shard_map/psum | solution.py:36
  1183.5 16.3 psum.131
  1201.2 113.1 %all-gather.13.cloned.1.call-done = f32[32768,64]{0,1:T(8,128)} async-done(((f32[128,64]{0,1:T(8,128)}), f32[32768,64]{0,1:T(8,128)}) %all-gather.13.cloned.1.call-update) | async-done | bytes 8388624 | tf_op jit(solution)/shard_map/all_gather | solution.py:46
  1314.3 4.9 copy.67
  1323.7 4.1 fusion.2
  1330.3 43.5 %all-reduce.15.cloned.1.call-done = f32[64,256]{1,0:T(8,128)} async-done(((f32[64,256]{1,0:T(8,128)}), f32[64,256]{1,0:T(8,128)}) %all-reduce.15.cloned.1.call-update) | async-done | bytes 65552 | tf_op jit(solution)/shard_map/psum | solution.py:31
  1378.5 4.9 fusion
  1383.5 231.3 %all-reduce = (f32[56,64]{1,0:T(8,128)S(1)}, f32[64,64]{0,1:T(8,128)S(1)}) all-reduce(f32[56,64]{1,0:T(8,128)S(1)} %bitcast.217, f32[64,64]{0,1:T(8,128)S(1)} %fusion.110), channel_id=1, replica_groups=mesh['pix'=64,'band'=4] {'pix'}, use_global_device_ids=true, to_apply=%region_40.0 | all-reduce | flops 7680 | bytes 61440 | tf_op jit(solution)/shard_map/psum | solution.py:36
  1619.3 16.0 psum.135
  1636.5 113.7 %all-gather.15.cloned.1.call-done = f32[32768,64]{0,1:T(8,128)} async-done(((f32[128,64]{0,1:T(8,128)}), f32[32768,64]{0,1:T(8,128)}) %all-gather.15.cloned.1.call-update) | async-done | bytes 8388624 | tf_op jit(solution)/shard_map/all_gather | solution.py:46
  1750.2 4.9 copy.68
  (128 shorter events, 55.1 us)
Async XLA Ops:
  7.2 58.8 %all-reduce.9.cloned.1.call-start = ((), (), s32[]{:S(2)}) async-start(), calls=%async_computation | async-start | bytes 131072 | tf_op jit(solution)/shard_map/psum | solution.py:31
  10.7 1.8 copy-start.3
  12.5 4.8 copy-start.13
  12.5 5.0 copy-start.12
  12.5 53.4 %copy-start.15 = (f32[64,256]{1,0:T(8,128)S(1)}, f32[64,256]{1,0:T(8,128)}, u32[]{:S(2)}) copy-start(f32[64,256]{1,0:T(8,128)} %param.5) | copy-start | bytes 196612
  17.3 425.3 %all-gather.9.cloned.1.call-start = ((), (), s32[]{:S(2)}) async-start(), calls=%async_computation.4 | async-start | bytes 8421376 | tf_op jit(solution)/shard_map/all_gather | solution.py:46
  65.9 4.7 copy-start.4
  311.4 190.6 %all-reduce.11.cloned.1.call-start = ((), (), s32[]{:S(2)}) async-start(), calls=%async_computation.1 | async-start | bytes 131072 | tf_op jit(solution)/shard_map/psum | solution.py:31
  447.4 2.0 copy-start
  450.1 1.8 copy-start.5
  456.7 421.8 %all-gather.11.cloned.1.call-start = ((), (), s32[]{:S(2)}) async-start(), calls=%async_computation.5 | async-start | bytes 8421376 | tf_op jit(solution)/shard_map/all_gather | solution.py:46
  502.0 4.7 copy-start.6
  747.3 190.6 %all-reduce.13.cloned.1.call-start = ((), (), s32[]{:S(2)}) async-start(), calls=%async_computation.2 | async-start | bytes 131072 | tf_op jit(solution)/shard_map/psum | solution.py:31
  883.3 2.0 copy-start.1
  886.0 1.8 copy-start.7
  892.5 421.8 %all-gather.13.cloned.1.call-start = ((), (), s32[]{:S(2)}) async-start(), calls=%async_computation.6 | async-start | bytes 8421376 | tf_op jit(solution)/shard_map/all_gather | solution.py:46
  937.8 4.7 copy-start.8
  1183.1 190.6 %all-reduce.15.cloned.1.call-start = ((), (), s32[]{:S(2)}) async-start(), calls=%async_computation.3 | async-start | bytes 131072 | tf_op jit(solution)/shard_map/psum | solution.py:31
  1319.2 2.0 copy-start.2
  1321.9 1.8 copy-start.9
  1328.4 421.8 %all-gather.15.cloned.1.call-start = ((), (), s32[]{:S(2)}) async-start(), calls=%async_computation.7 | async-start | bytes 8421376 | tf_op jit(solution)/shard_map/all_gather | solution.py:46
  1373.7 4.7 copy-start.10
  1375.0 8.4 copy-start.11
  1616.3 138.8 %copy-start.14 = (f32[56,64]{1,0:T(8,128)}, f32[56,64]{1,0:T(8,128)S(1)}, u32[]{:S(2)}) copy-start(f32[56,64]{1,0:T(8,128)S(1)} %fusion.55) | copy-start | bytes 43012
Sparse Core Ops, SparseCore 0:
  17.4 48.4 all-reduce.8
  311.5 131.0 all-gather.8
  456.8 45.1 all-reduce.10
  747.4 131.0 all-gather.10
  892.7 45.1 all-reduce.12
  1183.3 131.0 all-gather.12
  1328.5 45.1 all-reduce.14
  1619.2 131.0 all-gather.14
